TPU v7x, 512 devices: a whole 4x8x8 slice. The times are simulated.
512 devices in a mesh: row: 32 (over z, y_hi), col: 16 (over y_lo, x, core).
Axes of the slice: x: 4, y: 8 (y_hi: 4, y_lo: 2; y = y_hi * 2 + y_lo), z: 8, core: 2. Of those that a mesh axis runs over, the one named last changes fastest.
Arguments:
- signal: float32 [32, 65536], P(None, 'row'), may hold values from -8 to 8
- tile_values: bfloat16 [32, 16, 64, 128, 128], P('row', 'col'), may hold values from 1e-12 to 1, as said below
- tile_places: int32 [32, 16, 2, 64], P('row', 'col'), may hold values from 0 to 31, as said below
- tile_counts: int32 [32, 16], P('row', 'col'), may hold values from 16 to 64, as said below
Outputs:
- first_wavelet: float32 [32, 65536], P(None, 'row')
- second_wavelet: float32 [32, 65536], P(None, 'row')
- lowpass: float32 [32, 65536], P(None, 'row')
Inputs may be any that keep to these rules, and one draw needn't show every extreme that they name: `tile_values`: A is symmetric, and every node's row of A has a positive entry on the diagonal. Slots at or after a device's count hold tiles that are not part of A. `tile_places`: place 0 lies below 16, place 1 below 32; the live slots of one device name distinct places. `tile_counts`: some device is full in every draw.
All inputs are finite; a program needn't handle non-finite values.
Results may differ from a plain program's by a relative error of at most 0.0003.
Values may be sent and summed in bfloat16 or wider, within the bound.
No kernel may reach another device: no remote copies, remote signals or barrier semaphores. Data moves between devices by JAX's collectives and lax.ppermute only.
A program may use at most 64 MiB of HBM per device.

v0:
```python
import jax
import jax.numpy as jnp
from jax import lax
from jax.sharding import PartitionSpec as P

highest_precision = lax.Precision.HIGHEST


def broadcast(block, axis, holder):
    block = jnp.where(lax.axis_index(axis) == holder, block, jnp.zeros_like(block))
    return lax.psum(block, axis)


def on_device(signal, tile_values, tile_places, tile_counts):
    channels, row_len = signal.shape
    slot_count = tile_values.shape[2]
    tile_width = tile_values.shape[3]
    tile_rows = row_len // tile_width
    row_size = lax.axis_size("row")
    col_size = lax.axis_size("col")
    halves = row_size // col_size
    blocks = tile_values.reshape(slot_count, tile_width, tile_width)
    places = tile_places.reshape(2, slot_count)
    live_count = tile_counts.reshape(())
    live_slot = (lax.iota(jnp.int32, slot_count) < live_count).astype(jnp.float32)
    row_hot = (places[0][:, None] == lax.iota(jnp.int32, tile_rows)[None, :]).astype(
        jnp.float32
    ) * live_slot[:, None]

    def over_slots(partial_of):
        return partial_of(0, slot_count)

    def degree_part(start, size):
        sums = jnp.sum(blocks, axis=2, dtype=jnp.float32)
        return jnp.einsum("kt,ka->ta", row_hot, sums, precision=highest_precision)

    degree = lax.psum(over_slots(degree_part).reshape(row_len), "col")

    def walk(vector):
        scaled = (vector / degree[None, :]).astype(jnp.bfloat16)
        col_index = lax.axis_index("col")
        pieces = []
        for portion in range(halves):
            pieces.append(broadcast(scaled, "row", col_index * halves + portion))
        column = jnp.concatenate(pieces, axis=1).reshape(channels, halves * tile_rows, tile_width)

        def row_part(start, size):
            picked = jnp.take(column, places[1], axis=1)
            products = jnp.einsum(
                "kab,ckb->cka", blocks, picked, preferred_element_type=jnp.float32
            )
            return jnp.einsum("cka,kt->cta", products, row_hot, precision=highest_precision)

        partial_value = over_slots(row_part)
        spread = lax.psum(partial_value.reshape(channels, row_len), "col")
        return 0.5 * (vector + spread)

    walked = walk(signal)
    lowpass = walk(walked)
    return (jnp.abs(signal - walked), jnp.abs(walked - lowpass), lowpass)


def solution(mesh):
    in_specs = (
        P(None, "row"),
        P("row", "col", None, None, None),
        P("row", "col", None, None),
        P("row", "col"),
    )
    out_specs = (P(None, "row"), P(None, "row"), P(None, "row"))
    return jax.shard_map(
        on_device, mesh=mesh, in_specs=in_specs, out_specs=out_specs, check_vma=False
    )
```

profile of v0, /device:TPU:1, one launch (start us, length us, event | category | flops | bytes accessed | tf_op | source)
XLA Modules:
  0.0 942.9 jit_solution(6482408230794167764)
XLA Ops:
  7.2 0.0 copy-start.3
  7.2 0.0 copy-start.1
  7.2 0.0 all-reduce.13.cloned.1.call-start
  7.9 0.7 slice_bitcast_fusion
  8.6 0.0 copy-start
  8.6 2.4 convert_reduce_fusion
  11.0 0.1 convolution_bitcast_fusion
  11.1 33.8 %psum.49 = f32[2048]{0:T(1024)S(1)} all-reduce(f32[2048]{0:T(1024)S(1)} %convolution_bitcast_fusion), channel_id=1, replica_groups=mesh['row'=32,'col'=16] {'col'}, use_global_device_ids=true, to_apply=%region_1.0 | all-reduce | flops 2048 | bytes 16384 | tf_op jit(solution)/shard_map/psum | solution.py:37
  45.0 0.0 copy-done.1
  45.0 0.7 broadcast_select_fusion.3
  45.7 0.0 all-reduce.13.cloned.1.call-update
  45.7 0.0 all-reduce.7.cloned.1.call-start
  45.8 0.0 copy-done.3
  45.8 293.4 %all-reduce.13.cloned.1.call-done = (bf16[32,2048]{1,0:T(8,128)(2,1)}, bf16[32,2048]{1,0:T(8,128)(2,1)}) async-done(((bf16[32,2048]{1,0:T(8,128)(2,1)}, bf16[32,2048]{1,0:T(8,128)(2,1)}), (bf16[32,2048]{1,0:T(8,128)(2,1)}, bf16[32,2048]{1,0:T(8,128)(2,1)})) %all-reduce.13.cloned.1.call-update) | async-done | bytes 262160 | tf_op jit(solution)/shard_map/psum | solution.py:11
  339.2 1.0 copy_bitcast_fusion.3
  340.2 0.7 gather_fusion
  340.9 0.0 copy-done
  340.9 1.2 fusion.4
  342.1 1.2 fusion.12
  343.3 0.8 copy.24
  344.1 0.0 all-reduce.7.cloned.1.call-update
  344.1 0.0 all-reduce.11.cloned.1.call-start
  344.2 143.4 %all-reduce.7.cloned.1.call-done = f32[32,2048]{1,0:T(8,128)} async-done(((f32[32,2048]{1,0:T(8,128)}), f32[32,2048]{1,0:T(8,128)}) %all-reduce.7.cloned.1.call-update) | async-done | bytes 262160 | tf_op jit(solution)/shard_map/psum | solution.py:55
  487.5 1.7 broadcast_select_fusion.2
  489.2 0.7 broadcast_select_fusion
  489.9 0.0 all-reduce.11.cloned.1.call-update
  489.9 0.0 all-reduce.9.cloned.1.call-start
  489.9 296.2 %all-reduce.11.cloned.1.call-done = (bf16[32,2048]{1,0:T(8,128)(2,1)}, bf16[32,2048]{1,0:T(8,128)(2,1)}) async-done(((bf16[32,2048]{1,0:T(8,128)(2,1)}, bf16[32,2048]{1,0:T(8,128)(2,1)}), (bf16[32,2048]{1,0:T(8,128)(2,1)}, bf16[32,2048]{1,0:T(8,128)(2,1)})) %all-reduce.11.cloned.1.call-update) | async-done | bytes 262160 | tf_op jit(solution)/shard_map/psum | solution.py:11
  786.2 1.0 copy_bitcast_fusion.2
  787.2 0.7 gather_fusion.1
  787.8 0.0 copy-start.2
  787.8 1.2 fusion.7
  789.1 1.2 fusion.10
  790.3 0.8 copy.23
  791.1 0.0 all-reduce.9.cloned.1.call-update
  791.1 143.4 %all-reduce.9.cloned.1.call-done = f32[32,2048]{1,0:T(8,128)} async-done(((f32[32,2048]{1,0:T(8,128)}), f32[32,2048]{1,0:T(8,128)}) %all-reduce.9.cloned.1.call-update) | async-done | bytes 262160 | tf_op jit(solution)/shard_map/psum | solution.py:55
  934.5 0.0 copy-done.2
  934.5 1.9 subtract_abs_fusion
  (3 shorter events, 0.0 us)
Async XLA Ops:
  7.2 38.6 %copy-start.3 = (s32[1,1,2,64]{3,2,1,0:T(2,128)S(1)}, s32[1,1,2,64]{3,2,1,0:T(2,128)}, u32[]{:S(2)}) copy-start(s32[1,1,2,64]{3,2,1,0:T(2,128)} %param.8) | copy-start | bytes 1540
  7.2 37.8 %copy-start.1 = (f32[32,2048]{1,0:T(8,128)S(1)}, f32[32,2048]{1,0:T(8,128)}, u32[]{:S(2)}) copy-start(f32[32,2048]{1,0:T(8,128)} %param.6) | copy-start | bytes 786436
  7.2 332.0 %all-reduce.13.cloned.1.call-start = ((), (), s32[]{:S(2)}) async-start(), calls=%async_computation.3 | async-start | bytes 524288 | tf_op jit(solution)/shard_map/psum | solution.py:11
  8.6 332.3 %copy-start = (bf16[1,1,64,128,128]{4,3,2,1,0:T(8,128)(2,1)S(1)}, bf16[1,1,64,128,128]{4,3,2,1,0:T(8,128)(2,1)}, u32[]{:S(2)}) copy-start(bf16[1,1,64,128,128]{4,3,2,1,0:T(8,128)(2,1)} %param.7) | copy-start | bytes 6291460
  45.7 441.8 %all-reduce.7.cloned.1.call-start = ((), (), s32[]{:S(2)}) async-start(), calls=%async_computation | async-start | bytes 524288 | tf_op jit(solution)/shard_map/psum | solution.py:55
  344.1 442.0 %all-reduce.11.cloned.1.call-start = ((), (), s32[]{:S(2)}) async-start(), calls=%async_computation.2 | async-start | bytes 524288 | tf_op jit(solution)/shard_map/psum | solution.py:11
  489.9 444.6 %all-reduce.9.cloned.1.call-start = ((), (), s32[]{:S(2)}) async-start(), calls=%async_computation.1 | async-start | bytes 524288 | tf_op jit(solution)/shard_map/psum | solution.py:55
  787.8 146.6 %copy-start.2 = (f32[32,2048]{1,0:T(8,128)S(1)}, f32[32,2048]{1,0:T(8,128)}, u32[]{:S(2)}) copy-start(f32[32,2048]{1,0:T(8,128)} %all-reduce.7.cloned.1.call-done) | copy-start | bytes 786436
Sparse Core Ops, SparseCore 0:
  45.9 293.3 all-reduce.12
  344.3 143.2 all-reduce.6
  491.1 295.0 all-reduce.10
  791.2 143.2 all-reduce.8
where the time goes:
time: 943 us
  waiting for transfers between devices  876 us (93%)
  blocking collectives  33.8 us (4%)
  between operations  14.6 us (2%)
    psum x2, waiting for transfers between devices, broadcast(): return lax.psum(block, axis)  590 us
    psum x2, waiting for transfers between devices, walk(): spread = lax.psum(partial_value.reshape(channels, row_len), 'col')  287 us
    psum x1, blocking collectives, on_device(): degree = lax.psum(over_slots(degree_part).reshape(row_len), 'col')  33.8 us
  transfers between devices with their start and end apart: 4, of which 4 were waited for; matrix products, arithmetic and copies ran while one was open for 0% of the time, Pallas kernels for 0%

commit v1 on v0

v1 whole, which is shorter than its diff:
```python
import jax
import jax.numpy as jnp
from jax import lax
from jax.sharding import PartitionSpec as P

highest_precision = lax.Precision.HIGHEST


def column_perms(row_size, col_size):
    halves = row_size // col_size

    def flat(r, c):
        return r * col_size + c

    perms = []
    for shift in range(halves):
        pairs = []
        for c in range(col_size):
            for j in range(halves):
                for m in range(row_size // halves):
                    pairs.append((flat(halves * c + j, m), flat(halves * m + (j + shift) % halves, c)))
        perms.append(pairs)
    return perms


def on_device(signal, tile_values, tile_places, tile_counts):
    channels, row_len = signal.shape
    slot_count = tile_values.shape[2]
    tile_width = tile_values.shape[3]
    tile_rows = row_len // tile_width
    row_size = lax.axis_size("row")
    col_size = lax.axis_size("col")
    halves = row_size // col_size
    blocks = tile_values.reshape(slot_count, tile_width, tile_width)
    places = tile_places.reshape(2, slot_count)
    live_count = tile_counts.reshape(())
    live_slot = (lax.iota(jnp.int32, slot_count) < live_count).astype(jnp.float32)
    row_hot = (places[0][:, None] == lax.iota(jnp.int32, tile_rows)[None, :]).astype(
        jnp.float32
    ) * live_slot[:, None]
    perms = column_perms(row_size, col_size)
    parity = lax.axis_index("row") % halves
    col_tile = ((parity - places[1] // tile_rows) % halves) * tile_rows + places[1] % tile_rows

    sums = jnp.sum(blocks, axis=2, dtype=jnp.float32)
    degree_part = jnp.einsum("kt,ka->ta", row_hot, sums, precision=highest_precision)
    degree = lax.psum(degree_part.reshape(row_len), "col")

    def walk(vector):
        scaled = (vector / degree[None, :]).astype(jnp.bfloat16)
        pieces = [lax.ppermute(scaled, ("row", "col"), perm) for perm in perms]
        column = jnp.concatenate(pieces, axis=1).reshape(channels, halves * tile_rows, tile_width)
        picked = jnp.take(column, col_tile, axis=1)
        products = jnp.einsum(
            "kab,ckb->cka", blocks, picked, preferred_element_type=jnp.float32
        )
        partial_value = jnp.einsum("cka,kt->cta", products, row_hot, precision=highest_precision)
        spread = lax.psum(partial_value.reshape(channels, row_len), "col")
        return 0.5 * (vector + spread)

    walked = walk(signal)
    lowpass = walk(walked)
    return (jnp.abs(signal - walked), jnp.abs(walked - lowpass), lowpass)


def solution(mesh):
    in_specs = (
        P(None, "row"),
        P("row", "col", None, None, None),
        P("row", "col", None, None),
        P("row", "col"),
    )
    out_specs = (P(None, "row"), P(None, "row"), P(None, "row"))
    return jax.shard_map(
        on_device, mesh=mesh, in_specs=in_specs, out_specs=out_specs, check_vma=False
    )
```

time: 943 us -> 371 us (0.39)
  waiting for transfers between devices: 876 us -> 291 us
  starting transfers between devices: 0.16 us -> 16.5 us
    psum x2 -> x0, waiting for transfers between devices: 590 us -> none  [broadcast(): return lax.psum(block, axis)]
    ppermute x0 -> x4, starting transfers between devices: none -> 16.4 us  [walk(): pieces = [lax.ppermute(scaled, ('row', 'col'), perm) for perm in perms]]
    ppermute x0 -> x4, waiting for transfers between devices: none -> 13.8 us  [walk(): pieces = [lax.ppermute(scaled, ('row', 'col'), perm) for perm in perms]]
    psum x2, waiting for transfers between devices: 287 us -> 277 us  [walk(): spread = lax.psum(partial_value.reshape(channels, row_len), 'col')]
  transfers between devices with their start and end apart: 4 -> 6, of which waited for: 4 -> 5; matrix products, arithmetic and copies ran while one was open for 0% -> 0% of each run, Pallas kernels for 0% -> 0%
where the time goes in v1:
time: 371 us; the launch traced here: 370 us
  waiting for transfers between devices  291 us (78%)
  blocking collectives  33.8 us (9%)
  starting transfers between devices  16.5 us (4%)
  between operations  14.9 us (4%)
  other arithmetic  5.4 us (1%)
  matrix products  4.96 us (1%)
    psum x2, waiting for transfers between devices, walk(): spread = lax.psum(partial_value.reshape(channels, row_len), 'col')  277 us
    psum x1, blocking collectives, on_device(): degree = lax.psum(degree_part.reshape(row_len), 'col')  33.8 us
    ppermute x4, starting transfers between devices, walk(): pieces = [lax.ppermute(scaled, ('row', 'col'), perm) for perm in perms]  16.4 us
    ppermute x4, waiting for transfers between devices, walk(): pieces = [lax.ppermute(scaled, ('row', 'col'), perm) for perm in perms]  13.8 us
  transfers between devices with their start and end apart: 6, of which 5 were waited for; matrix products, arithmetic and copies ran while one was open for 0% of the time, Pallas kernels for 0%

profile of v1, /device:TPU:1, one launch (start us, length us, event | category | flops | bytes accessed | tf_op | source)
XLA Modules:
  0.0 370.3 jit_solution(13642957146635508868)
XLA Ops:
  7.2 0.0 copy-start.3
  7.2 0.0 copy-start.1
  7.2 0.0 all-reduce.3.cloned.1.call-start
  7.9 0.7 slice_bitcast_fusion
  8.6 0.0 copy-start
  8.6 2.4 convert_reduce_fusion
  11.0 0.1 convolution_bitcast_fusion
  11.1 33.8 %psum.21 = f32[2048]{0:T(1024)S(1)} all-reduce(f32[2048]{0:T(1024)S(1)} %convolution_bitcast_fusion), channel_id=1, replica_groups=mesh['row'=32,'col'=16] {'col'}, use_global_device_ids=true, to_apply=%region_1.2 | all-reduce | flops 2048 | bytes 16384 | tf_op jit(solution)/shard_map/psum | solution.py:47
  45.0 0.0 copy-done.1
  45.0 3.4 collective-permute-start.1
  48.4 3.5 collective-permute-start
  51.9 0.0 copy-done.3
  52.0 1.4 collective-permute-done.1
  53.4 5.3 %collective-permute-done = bf16[32,2048]{1,0:T(8,128)(2,1)S(1)} collective-permute-done((bf16[32,2048]{1,0:T(8,128)(2,1)S(1)}, bf16[32,2048]{1,0:T(8,128)(2,1)S(1)}, u32[]{:S(2)}, u32[]{:S(2)}) %collective-permute-start) | collective-permute-done | bytes 131104 | tf_op jit(solution)/shard_map/ppermute | solution.py:51
  58.7 0.7 gather_fusion
  59.4 0.0 copy-done
  59.4 1.2 fusion.4
  60.6 1.2 fusion.12
  61.8 0.8 copy.24
  62.6 0.0 all-reduce.3.cloned.1.call-update
  62.6 0.0 all-reduce.5.cloned.1.call-start
  62.7 139.6 %all-reduce.3.cloned.1.call-done = f32[32,2048]{1,0:T(8,128)} async-done(((f32[32,2048]{1,0:T(8,128)}), f32[32,2048]{1,0:T(8,128)}) %all-reduce.3.cloned.1.call-update) | async-done | bytes 262160 | tf_op jit(solution)/shard_map/psum | solution.py:58
  202.3 1.0 divide_convert_fusion
  203.3 5.6 %collective-permute-start.3 = (bf16[32,2048]{1,0:T(8,128)(2,1)S(1)}, bf16[32,2048]{1,0:T(8,128)(2,1)S(1)}, u32[]{:S(2)}, u32[]{:S(2)}) collective-permute-start(bf16[32,2048]{1,0:T(8,128)(2,1)S(1)} %divide_convert_fusion), channel_id=1, source_target_pairs={{0,16},{1,48},{2,80},{3,112},{4,144},{5,176},{6,208},{7,240},{8,27... | collective-permute-start | bytes 393224 | tf_op jit(solution)/shard_map/ppermute | solution.py:51
  208.9 4.0 %collective-permute-start.2 = (bf16[32,2048]{1,0:T(8,128)(2,1)S(1)}, bf16[32,2048]{1,0:T(8,128)(2,1)S(1)}, u32[]{:S(2)}, u32[]{:S(2)}) collective-permute-start(bf16[32,2048]{1,0:T(8,128)(2,1)S(1)} %divide_convert_fusion), channel_id=1, source_target_pairs={{0,0},{1,32},{2,64},{3,96},{4,128},{5,160},{6,192},{7,224},{8,256}... | collective-permute-start | bytes 393224 | tf_op jit(solution)/shard_map/ppermute | solution.py:51
  212.8 0.0 collective-permute-done.3
  212.8 7.1 %collective-permute-done.2 = bf16[32,2048]{1,0:T(8,128)(2,1)S(1)} collective-permute-done((bf16[32,2048]{1,0:T(8,128)(2,1)S(1)}, bf16[32,2048]{1,0:T(8,128)(2,1)S(1)}, u32[]{:S(2)}, u32[]{:S(2)}) %collective-permute-start.2) | collective-permute-done | bytes 131104 | tf_op jit(solution)/shard_map/ppermute | solution.py:51
  220.0 0.7 gather_fusion.1
  220.6 0.0 copy-start.2
  220.6 1.2 fusion.7
  221.9 1.2 fusion.10
  223.1 0.8 copy.23
  223.8 0.0 all-reduce.5.cloned.1.call-update
  223.9 137.7 %all-reduce.5.cloned.1.call-done = f32[32,2048]{1,0:T(8,128)} async-done(((f32[32,2048]{1,0:T(8,128)}), f32[32,2048]{1,0:T(8,128)}) %all-reduce.5.cloned.1.call-update) | async-done | bytes 262160 | tf_op jit(solution)/shard_map/psum | solution.py:58
  361.5 0.0 copy-done.2
  361.5 1.9 subtract_abs_fusion
  (6 shorter events, 0.2 us)
Async XLA Ops:
  7.2 44.7 %copy-start.3 = (s32[1,1,2,64]{3,2,1,0:T(2,128)S(1)}, s32[1,1,2,64]{3,2,1,0:T(2,128)}, u32[]{:S(2)}) copy-start(s32[1,1,2,64]{3,2,1,0:T(2,128)} %param.8) | copy-start | bytes 1540
  7.2 37.8 %copy-start.1 = (f32[32,2048]{1,0:T(8,128)S(1)}, f32[32,2048]{1,0:T(8,128)}, u32[]{:S(2)}) copy-start(f32[32,2048]{1,0:T(8,128)} %param.6) | copy-start | bytes 786436
  7.2 195.1 %all-reduce.3.cloned.1.call-start = ((), (), s32[]{:S(2)}) async-start(), calls=%async_computation | async-start | bytes 524288 | tf_op jit(solution)/shard_map/psum | solution.py:58
  8.6 50.8 %copy-start = (bf16[1,1,64,128,128]{4,3,2,1,0:T(8,128)(2,1)S(1)}, bf16[1,1,64,128,128]{4,3,2,1,0:T(8,128)(2,1)}, u32[]{:S(2)}) copy-start(bf16[1,1,64,128,128]{4,3,2,1,0:T(8,128)(2,1)} %param.7) | copy-start | bytes 6291460
  45.0 8.4 %collective-permute-start.1 = (bf16[32,2048]{1,0:T(8,128)(2,1)S(1)}, bf16[32,2048]{1,0:T(8,128)(2,1)S(1)}, u32[]{:S(2)}, u32[]{:S(2)}) collective-permute-start(bf16[32,2048]{1,0:T(8,128)(2,1)S(1)} %divide_convert_fusion.1), channel_id=1, source_target_pairs={{0,16},{1,48},{2,80},{3,112},{4,144},{5,176},{6,208},{7,240},{8,27... | collective-permute-start | bytes 393224 | tf_op jit(solution)/shard_map/ppermute | solution.py:51
  48.4 10.3 %collective-permute-start = (bf16[32,2048]{1,0:T(8,128)(2,1)S(1)}, bf16[32,2048]{1,0:T(8,128)(2,1)S(1)}, u32[]{:S(2)}, u32[]{:S(2)}) collective-permute-start(bf16[32,2048]{1,0:T(8,128)(2,1)S(1)} %divide_convert_fusion.1), channel_id=1, source_target_pairs={{0,0},{1,32},{2,64},{3,96},{4,128},{5,160},{6,192},{7,224},{8,256}... | collective-permute-start | bytes 393224 | tf_op jit(solution)/shard_map/ppermute | solution.py:51
  62.6 298.9 %all-reduce.5.cloned.1.call-start = ((), (), s32[]{:S(2)}) async-start(), calls=%async_computation.1 | async-start | bytes 524288 | tf_op jit(solution)/shard_map/psum | solution.py:58
  203.3 9.5 %collective-permute-start.3 = (bf16[32,2048]{1,0:T(8,128)(2,1)S(1)}, bf16[32,2048]{1,0:T(8,128)(2,1)S(1)}, u32[]{:S(2)}, u32[]{:S(2)}) collective-permute-start(bf16[32,2048]{1,0:T(8,128)(2,1)S(1)} %divide_convert_fusion), channel_id=1, source_target_pairs={{0,16},{1,48},{2,80},{3,112},{4,144},{5,176},{6,208},{7,240},{8,27... | collective-permute-start | bytes 393224 | tf_op jit(solution)/shard_map/ppermute | solution.py:51
  208.9 11.0 %collective-permute-start.2 = (bf16[32,2048]{1,0:T(8,128)(2,1)S(1)}, bf16[32,2048]{1,0:T(8,128)(2,1)S(1)}, u32[]{:S(2)}, u32[]{:S(2)}) collective-permute-start(bf16[32,2048]{1,0:T(8,128)(2,1)S(1)} %divide_convert_fusion), channel_id=1, source_target_pairs={{0,0},{1,32},{2,64},{3,96},{4,128},{5,160},{6,192},{7,224},{8,256}... | collective-permute-start | bytes 393224 | tf_op jit(solution)/shard_map/ppermute | solution.py:51
  220.6 140.9 %copy-start.2 = (f32[32,2048]{1,0:T(8,128)S(1)}, f32[32,2048]{1,0:T(8,128)}, u32[]{:S(2)}) copy-start(f32[32,2048]{1,0:T(8,128)} %all-reduce.3.cloned.1.call-done) | copy-start | bytes 786436
Sparse Core Ops, SparseCore 0:
  62.8 139.5 all-reduce.2
  224.0 137.4 all-reduce.4
